TPU v7x, 32 devices: a whole 2x2x4 slice. The times are simulated.
32 devices in a mesh: groups: 2 (over x), dp: 8 (over z, y), mp: 2 (over core).
Axes of the slice: x: 2, y: 2, z: 4, core: 2. Of those that a mesh axis runs over, the one named last changes fastest.
Arguments:
- residual: bfloat16 [48, 128, 8192], P(('groups', 'dp'), None, 'mp'), parts along dimension 0
- lengths: int32 [48], P(('groups', 'dp')), parts along dimension 0, may hold values from 32 to 128
- labels: int32 [48], P(('groups', 'dp')), parts along dimension 0, may hold values from 0 to 1, as said below
- earlier_means: float32 [16, 79, 2, 8192], P(('groups', 'dp'), None, None, 'mp'), parts along dimension 0
- chosen: int32 [2], P('groups'), parts along dimension 0, may hold values from 0 to 79
- norm_gain: float32 [8192], P('mp'), may hold values from 0.1 to 1.9
- key_weight: bfloat16 [2, 4096, 1024], P('mp', 'dp'), may hold values from -0.0625 to 0.0625
- value_weight: bfloat16 [2, 4096, 1024], P('mp', 'dp'), may hold values from -0.0625 to 0.0625
- out_proj: bfloat16 [2, 8192, 8192], P('groups', 'mp', 'dp'), parts along dimension 0
Outputs:
- directions: float32 [160, 8192], P('groups', 'mp'), parts along dimension 0
- key_cache: bfloat16 [48, 128, 1024], P(('groups', 'dp'), None, 'mp'), parts along dimension 0
- value_cache: bfloat16 [48, 128, 1024], P(('groups', 'dp'), None, 'mp'), parts along dimension 0
- ortho_proj: bfloat16 [2, 8192, 8192], P('groups', 'mp', 'dp'), parts along dimension 0
There are 2 independent parts, one for each index of `groups`. A program takes and returns all parts, laid end to end along the dimension named above; an argument that names none is the same for every part. Nothing has to cross between parts.
Inputs may be any that keep to these rules, and one draw needn't show every extreme that they name: Every slab of 3 consecutive prompts holds both labels.
All inputs are finite; a program needn't handle non-finite values.
Results may differ from a plain program's by a relative error of at most 0.0051.
Values may be sent and summed in bfloat16 or wider, within the bound.
A program may use at most 384 MiB of HBM per device.

v0:
```python
import math
import jax
import jax.numpy as jnp
from jax import lax
from jax.sharding import PartitionSpec as P


def direction_parts(residual, lengths, labels, earlier_means, chosen):
    highest = lax.Precision.HIGHEST
    length = residual.shape[1]
    positions = jnp.arange(length, dtype=jnp.int32)
    valid_mask = (positions[None, :] < lengths[:, None]).astype(jnp.bfloat16)
    masked_sums = jnp.einsum("pt,ptd->pd", valid_mask, residual, preferred_element_type=jnp.float32)
    prompt_mean = masked_sums / lengths.astype(jnp.float32)[:, None]
    onehot = (labels[:, None] == jnp.arange(2, dtype=jnp.int32)[None, :]).astype(jnp.float32)
    counts = jnp.sum(onehot, axis=0)
    current = jnp.sum(onehot[:, :, None] * prompt_mean[:, None, :], axis=0) / counts[:, None]
    earlier = earlier_means[0]
    layers = earlier.shape[0] + 1
    picked = lax.dynamic_index_in_dim(
        earlier, jnp.minimum(chosen[0], layers - 2), 0, keepdims=False
    )
    picked = jnp.where(chosen[0] == layers - 1, current, picked)
    weighted, totals = lax.psum((counts[:, None] * picked, counts), "dp")
    merged = weighted / totals[:, None]
    picked_difference = merged[1] - merged[0]
    share = counts / totals
    local = jnp.concatenate(
        [
            share[1] * earlier[:, 1] - share[0] * earlier[:, 0],
            (share[1] * current[1] - share[0] * current[0])[None],
        ],
        axis=0,
    )
    return (picked_difference, local)


def shards(
    residual, lengths, labels, earlier_means, chosen, norm_gain, key_weight, value_weight, out_proj
):
    highest = lax.Precision.HIGHEST
    prompts, length, half_width = residual.shape
    model_width = half_width * lax.axis_size("mp")
    picked_difference, local = direction_parts(residual, lengths, labels, earlier_means, chosen)
    key_full = lax.all_gather(key_weight, "dp", axis=1, tiled=True)[0]
    value_full = lax.all_gather(value_weight, "dp", axis=1, tiled=True)[0]
    difference = lax.psum(local, "dp")
    square_sums = lax.psum(jnp.sum(difference * difference, axis=1), "mp")
    directions = difference * lax.rsqrt(square_sums / model_width + 1e-06)[:, None]
    local_square = jnp.sum(picked_difference * picked_difference)
    local_mean = local_square / half_width + 1e-06
    unit = picked_difference * lax.rsqrt(local_mean)
    token_rows = residual.reshape(prompts * length, half_width)
    row_values = token_rows.astype(jnp.float32)
    matrix = out_proj[0]
    dots = jnp.sum(row_values * unit[None, :], axis=1)
    columns = jnp.sum(matrix.astype(jnp.float32) * unit[:, None], axis=0)
    packed = jnp.concatenate([dots, columns, local_square[None]])
    pieces = lax.all_gather(packed, "mp")
    squares = pieces[:, -1]
    mean_dir = jnp.sum(squares) / model_width + 1e-06
    ratios = jnp.sqrt((squares / half_width + 1e-06) / mean_dir) / math.sqrt(model_width)
    sums = jnp.sum(pieces * ratios[:, None], axis=0)
    projection = sums[: prompts * length]
    column_proj = sums[prompts * length : -1]
    refusal_dir = picked_difference * (lax.rsqrt(mean_dir) / math.sqrt(model_width))
    ablated = row_values - projection[:, None] * refusal_dir[None, :]
    mean_square = lax.psum(jnp.sum(ablated * ablated, axis=1), "mp") / model_width
    normed = (ablated * lax.rsqrt(mean_square + 1e-05)[:, None] * norm_gain[None, :]).astype(
        jnp.bfloat16
    )
    ortho_proj = (matrix.astype(jnp.float32) - refusal_dir[:, None] * column_proj[None, :]).astype(
        jnp.bfloat16
    )[None]
    key_sum = jnp.dot(normed, key_full, preferred_element_type=jnp.float32)
    value_sum = jnp.dot(normed, value_full, preferred_element_type=jnp.float32)
    key_sums, value_sums = (
        lax.psum_scatter(key_sum, "mp", scatter_dimension=1, tiled=True),
        lax.psum_scatter(value_sum, "mp", scatter_dimension=1, tiled=True),
    )
    key_cache = key_sums.astype(jnp.bfloat16).reshape(prompts, length, key_sums.shape[1])
    value_cache = value_sums.astype(jnp.bfloat16).reshape(prompts, length, value_sums.shape[1])
    return (directions, key_cache, value_cache, ortho_proj)


def solution(mesh):
    return jax.shard_map(
        shards,
        mesh=mesh,
        in_specs=(
            P(("groups", "dp"), None, "mp"),
            P(("groups", "dp")),
            P(("groups", "dp")),
            P(("groups", "dp"), None, None, "mp"),
            P("groups"),
            P("mp"),
            P("mp", "dp", None),
            P("mp", "dp", None),
            P("groups", "mp", "dp"),
        ),
        out_specs=(
            P("groups", "mp"),
            P(("groups", "dp"), None, "mp"),
            P(("groups", "dp"), None, "mp"),
            P("groups", "mp", "dp"),
        ),
        check_vma=False,
    )
```

profile of v0, /device:TPU:0, one launch (start us, length us, event | category | flops | bytes accessed | tf_op | source)
XLA Modules:
  0.0 425.7 jit_solution(17136357276199874435)
XLA Ops:
  7.2 0.0 copy-start
  7.2 0.0 all-reduce.5.cloned.1.call-start
  7.2 0.9 fusion.14
  8.1 0.7 convert_element_type.46
  8.8 0.8 fusion.15
  9.6 0.7 compare_convert_fusion
  10.9 0.1 copy.17
  11.0 4.7 %copy.24 = f32[1,79,2,4096]{3,1,2,0:T(8,128)} copy(f32[1,79,2,4096]{3,2,1,0:T(2,128)} %param.12) | data formatting | bytes 5177344 | tf_op args[3]
  15.7 0.0 copy-done
  15.7 0.5 fusion.12
  16.2 0.1 bitcast_divide_fusion
  16.3 0.1 multiply_reduce_fusion.2
  16.4 0.9 fusion.10
  17.3 39.2 %all-reduce.1 = (f32[2]{0:T(128)S(1)}, f32[2,4096]{1,0:T(2,128)S(1)}) all-reduce(f32[2]{0:T(128)S(1)} %fusion.15, f32[2,4096]{1,0:T(2,128)S(1)} %get-tuple-element.10), channel_id=1, replica_groups=mesh['groups'=2,'dp'=8,'mp'=2] {'dp'}, use_global_device_ids=true, to_apply=%region_1.0 | all-reduce | flops 8194 | bytes 65552 | tf_op jit(solution)/shard_map/psum | solution.py:24
  56.5 0.6 fusion.16
  57.0 1.3 fusion.11
  58.4 3.1 fusion.9
  61.5 0.0 copy-start.4
  61.5 1.2 pad_maximum_fusion
  62.7 0.0 all-reduce.5.cloned.1.call-update
  62.7 0.0 all-gather.4.cloned.1.call-start
  62.8 0.7 all-gather.4.cloned.1.call-update
  63.5 0.0 all-gather.6.cloned.1.call-start
  63.5 0.7 all-gather.6.cloned.1.call-update
  64.2 0.0 reduce-scatter.3.cloned.1.call-start
  64.3 0.1 broadcast_divide_fusion
  64.3 0.6 multiply_reduce_fusion.3
  65.7 0.0 copy-done.4
  65.7 0.6 dynamic-slice.1
  67.0 0.7 fusion.7
  67.7 5.1 %fusion.1 = f32[1024]{0:T(1024)S(1)} fusion(bf16[1,4096,1024]{2,1,0:T(8,128)(2,1)} %param.17, f32[4096]{0:T(1024)S(1)} %bitcast.54), kind=kLoop, calls=%fused_computation.3 | loop fusion | flops 12581888 | bytes 8409088 | tf_op jit(solution)/shard_map/reduce_sum | solution.py:57
  72.8 0.0 copy-start.3
  72.8 0.8 maximum_dynamic-update-slice_fusion
  73.6 3.3 all-reduce
  76.8 0.1 reshape.183
  76.9 0.6 slice_reduce_fusion
  78.2 0.1 multiply_reduce_fusion.5
  78.3 0.1 multiply_reduce_fusion.4
  78.5 1.2 multiply_reduce_fusion
  79.7 63.7 %all-reduce.5.cloned.1.call-done = f32[80,4096]{1,0:T(8,128)} async-done(((f32[80,4096]{1,0:T(8,128)}), f32[80,4096]{1,0:T(8,128)}) %all-reduce.5.cloned.1.call-update) | async-done | bytes 1310736 | tf_op jit(solution)/shard_map/psum | solution.py:47
  143.4 1.5 multiply_reduce_fusion.1
  144.9 2.5 all-reduce.2
  147.4 0.0 copy-done.3
  147.4 3.4 multiply_convert_fusion
  150.8 119.1 %all-gather.4.cloned.1.call-done = bf16[1,4096,1024]{2,1,0:T(8,128)(2,1)} async-done(((bf16[1,512,1024]{2,1,0:T(8,128)(2,1)}), bf16[1,4096,1024]{2,1,0:T(8,128)(2,1)}) %all-gather.4.cloned.1.call-update) | async-done | bytes 8388624 | tf_op jit(solution)/shard_map/all_gather | solution.py:45
  269.9 0.0 copy-start.2
  269.9 9.0 %fusion.5 = f32[384,1024]{1,0:T(8,128)} fusion(bf16[384,4096]{1,0:T(8,128)(2,1)} %bitcast.46, bf16[1,4096,1024]{2,1,0:T(8,128)(2,1)} %all-gather.4.cloned.1.call-done), kind=kOutput, calls=%fused_computation.7 | convolution fusion | flops 3221225472 | bytes 13107200 | tf_op jit(solution)/shard_map/dot_general | solution.py:75
  278.9 0.0 reduce-scatter.3.cloned.1.call-update
  279.0 0.0 reduce-scatter.5.cloned.1.call-start
  279.0 116.4 %all-gather.6.cloned.1.call-done = bf16[1,4096,1024]{2,1,0:T(8,128)(2,1)} async-done(((bf16[1,512,1024]{2,1,0:T(8,128)(2,1)}), bf16[1,4096,1024]{2,1,0:T(8,128)(2,1)}) %all-gather.6.cloned.1.call-update) | async-done | bytes 8388624 | tf_op jit(solution)/shard_map/all_gather | solution.py:46
  395.4 0.0 copy-done.2
  395.4 7.0 %fusion.3 = f32[384,1024]{1,0:T(8,128)} fusion(bf16[384,4096]{1,0:T(8,128)(2,1)S(1)} %bitcast.47, bf16[1,4096,1024]{2,1,0:T(8,128)(2,1)} %all-gather.6.cloned.1.call-done), kind=kOutput, calls=%fused_computation.5 | convolution fusion | flops 3221225472 | bytes 13107200 | tf_op jit(solution)/shard_map/dot_general | solution.py:76
  402.4 0.0 reduce-scatter.5.cloned.1.call-update
  402.4 0.0 copy-start.1
  402.5 8.0 %fusion.2 = bf16[1,4096,1024]{2,1,0:T(8,128)(2,1)} fusion(bf16[1,4096,1024]{2,1,0:T(8,128)(2,1)} %param.17, f32[1024]{0:T(1024)S(1)} %slice.54, f32[4096]{0:T(1024)S(1)} %bitcast.52), kind=kLoop, calls=%fused_computation.4 | loop fusion | flops 16777216 | bytes 16797696 | tf_op jit(solution)/shard_map/convert_element_type | solution.py:72
  410.5 0.0 copy-done.1
  410.5 1.2 broadcast_multiply_fusion
  411.7 0.0 reduce-scatter.3.cloned.1.call-done
  411.7 1.9 convert_element_type.52
  413.7 3.6 reduce-scatter.5.cloned.1.call-done
  417.2 1.9 convert_element_type.53
  (8 shorter events, 0.1 us)
Async XLA Ops:
  7.2 8.5 %copy-start = (bf16[3,128,4096]{2,1,0:T(8,128)(2,1)S(1)}, bf16[3,128,4096]{2,1,0:T(8,128)(2,1)}, u32[]{:S(2)}) copy-start(bf16[3,128,4096]{2,1,0:T(8,128)(2,1)} %param.9) | copy-start | bytes 9437188
  7.2 136.2 %all-reduce.5.cloned.1.call-start = ((), (), s32[]{:S(2)}) async-start(), calls=%async_computation.2 | async-start | bytes 2621440 | tf_op jit(solution)/shard_map/psum | solution.py:47
  61.5 4.2 copy-start.4
  62.7 207.2 %all-gather.4.cloned.1.call-start = ((), (), s32[]{:S(2)}) async-start(), calls=%async_computation.3 | async-start | bytes 9437184 | tf_op jit(solution)/shard_map/all_gather | solution.py:45
  63.5 331.9 %all-gather.6.cloned.1.call-start = ((), (), s32[]{:S(2)}) async-start(), calls=%async_computation.5 | async-start | bytes 9437184 | tf_op jit(solution)/shard_map/all_gather | solution.py:46
  64.2 347.5 %reduce-scatter.3.cloned.1.call-start = ((), (), s32[]{:S(2)}) async-start(), calls=%async_computation.4 | async-start | bytes 2359296 | tf_op jit(solution)/shard_map/reduce_scatter | solution.py:78
  72.8 74.6 %copy-start.3 = (f32[4096]{0:T(1024)S(1)}, f32[4096]{0:T(1024)}, u32[]{:S(2)}) copy-start(f32[4096]{0:T(1024)} %param.14) | copy-start | bytes 49156
  269.9 125.5 %copy-start.2 = (bf16[3,128,4096]{2,1,0:T(8,128)(2,1)S(1)}, bf16[3,128,4096]{2,1,0:T(8,128)(2,1)}, u32[]{:S(2)}) copy-start(bf16[3,128,4096]{2,1,0:T(8,128)(2,1)} %multiply_convert_fusion) | copy-start | bytes 9437188
  279.0 138.3 %reduce-scatter.5.cloned.1.call-start = ((), (), s32[]{:S(2)}) async-start(), calls=%async_computation.6 | async-start | bytes 2359296 | tf_op jit(solution)/shard_map/reduce_scatter | solution.py:79
  402.4 8.0 %copy-start.1 = (f32[80,4096]{1,0:T(8,128)S(1)}, f32[80,4096]{1,0:T(8,128)}, u32[]{:S(2)}) copy-start(f32[80,4096]{1,0:T(8,128)} %all-reduce.5.cloned.1.call-done) | copy-start | bytes 3932164
Sparse Core Ops, SparseCore 0:
  62.8 80.5 all-reduce.4
  145.7 124.1 all-gather.3
  272.2 123.1 all-gather.5
  397.6 7.2 reduce-scatter.2
  406.9 10.2 reduce-scatter.4
where the time goes:
time: 426 us
  waiting for transfers between devices  304 us (71%)
  blocking collectives  44.9 us (11%)
  other arithmetic  37 us (9%)
  between operations  16.7 us (4%)
  matrix products  16.6 us (4%)
  local copies, waits for them, and re-layouts  6.11 us (1%)
    all_gather x1, waiting for transfers between devices, shards(): key_full = lax.all_gather(key_weight, 'dp', axis=1, tiled=True)[0]  119 us
    all_gather x1, waiting for transfers between devices, shards(): value_full = lax.all_gather(value_weight, 'dp', axis=1, tiled=True)[0]  116 us
    psum x1, waiting for transfers between devices, shards(): difference = lax.psum(local, 'dp')  63.7 us
    psum x1, blocking collectives, direction_parts(): weighted, totals = lax.psum((counts[:, None] * picked, counts), 'dp')  39.2 us
    dot_general x1, matrix products, shards(): key_sum = jnp.dot(normed, key_full, preferred_element_type=jnp.float32)  9.04 us
  transfers between devices with their start and end apart: 5, of which 4 were waited for; matrix products, arithmetic and copies ran while one was open for 10% of the time, Pallas kernels for 0%

commit v1 on v0

--- a/solution.py
+++ b/solution.py
@@ -1,8 +1,29 @@
+import functools
 import math
 import jax
 import jax.numpy as jnp
 from jax import lax
 from jax.sharding import PartitionSpec as P
+
+
+def step_on_task_over_axis(target, join_dim):
+    dev_count = lax.psum(1, "dp")
+    arrivals = [(it, (it + 1) % dev_count) for it in range(dev_count)]
+    so_far_all = [(it, (it - 1) % dev_count) for it in range(dev_count)]
+    vec_out, back = ([target], [target])
+    for _ in range(dev_count // 2):
+        g_now = lax.ppermute(vec_out[-1], "dp", arrivals)
+        vec_out.append(g_now)
+    for _ in range((dev_count - 1) // 2):
+        back.append(lax.ppermute(back[-1], "dp", so_far_all))
+    a_next = jnp.concatenate([*vec_out[::-1], *back[1:]], axis=join_dim)
+    parts_out = jnp.roll(
+        a_next, (lax.axis_index("dp") - dev_count // 2) * target.shape[join_dim], axis=join_dim
+    )
+    return parts_out
+
+
+_supply_weights = functools.partial(step_on_task_over_axis, join_dim=1)
 
 
 def direction_parts(residual, lengths, labels, earlier_means, chosen):
@@ -42,7 +63,7 @@
     prompts, length, half_width = residual.shape
     model_width = half_width * lax.axis_size("mp")
     picked_difference, local = direction_parts(residual, lengths, labels, earlier_means, chosen)
-    key_full = lax.all_gather(key_weight, "dp", axis=1, tiled=True)[0]
+    key_full = _supply_weights(key_weight)[0]
     value_full = lax.all_gather(value_weight, "dp", axis=1, tiled=True)[0]
     difference = lax.psum(local, "dp")
     square_sums = lax.psum(jnp.sum(difference * difference, axis=1), "mp")

time: 426 us -> 393 us (0.923)
  waiting for transfers between devices: 304 us -> 224 us
  starting transfers between devices: 0.2 us -> 36.1 us
  local copies, waits for them, and re-layouts: 6.11 us -> 19.6 us
    all_gather x1 -> x0, waiting for transfers between devices: 119 us -> none  [shards(): key_full = lax.all_gather(key_weight, 'dp', axis=1, tiled=True)[0]]
    ppermute x0 -> x7, waiting for transfers between devices: none -> 102 us  [the longest x4 102 us: step_on_task_over_axis(): g_now = lax.ppermute(vec_out[-1], 'dp', arrivals)]
    all_gather x1, waiting for transfers between devices: 116 us -> 69.2 us  [shards(): value_full = lax.all_gather(value_weight, 'dp', axis=1, tiled=True)[0]]
    ppermute x0 -> x7, starting transfers between devices: none -> 35.9 us  [the longest x3 30.9 us: step_on_task_over_axis(): back.append(lax.ppermute(back[-1], 'dp', so_far_all))]
    psum x1, waiting for transfers between devices: 63.7 us -> 49.5 us  [shards(): difference = lax.psum(local, 'dp')]
    unnamed x13 -> x30, local copies, waits for them, and re-layouts: 5.34 us -> 18.8 us
    dot_general x1, matrix products: 9.04 us -> 4.71 us  [shards(): key_sum = jnp.dot(normed, key_full, preferred_element_type=jnp.float32)]
  transfers between devices with their start and end apart: 5 -> 11, of which waited for: 4 -> 6; matrix products, arithmetic and copies ran while one was open for 10% -> 13% of each run, Pallas kernels for 0% -> 0%
where the time goes in v1:
time: 393 us; the launch traced here: 392 us
  waiting for transfers between devices  224 us (57%)
  blocking collectives  44.9 us (11%)
  starting transfers between devices  36.1 us (9%)
  other arithmetic  35.3 us (9%)
  local copies, waits for them, and re-layouts  19.6 us (5%)
  between operations  16.8 us (4%)
  matrix products  16 us (4%)
    ppermute x4, waiting for transfers between devices, step_on_task_over_axis(): g_now = lax.ppermute(vec_out[-1], 'dp', arrivals)  102 us
    all_gather x1, waiting for transfers between devices, shards(): value_full = lax.all_gather(value_weight, 'dp', axis=1, tiled=True)[0]  69.2 us
    psum x1, waiting for transfers between devices, shards(): difference = lax.psum(local, 'dp')  49.5 us
    psum x1, blocking collectives, direction_parts(): weighted, totals = lax.psum((counts[:, None] * picked, counts), 'dp')  39.2 us
    ppermute x3, starting transfers between devices, step_on_task_over_axis(): back.append(lax.ppermute(back[-1], 'dp', so_far_all))  30.9 us
    unnamed x30, local copies, waits for them, and re-layouts  18.8 us
    dot_general x1, matrix products, shards(): value_sum = jnp.dot(normed, value_full, preferred_element_type=jnp.float32)  8.89 us
    convert_element_type x1, other arithmetic, shards(): (matrix.astype(jnp.float32) - refusal_dir[:, None] * column_proj[None, :]...  7.97 us
  transfers between devices with their start and end apart: 11, of which 6 were waited for; matrix products, arithmetic and copies ran while one was open for 13% of the time, Pallas kernels for 0%

profile of v1, /device:TPU:0, one launch (start us, length us, event | category | flops | bytes accessed | tf_op | source)
XLA Modules:
  0.0 392.2 jit_solution(14584390844650771717)
XLA Ops:
  7.2 0.7 fusion.15
  7.9 0.7 convert_element_type.46
  8.6 0.8 fusion.17
  9.4 0.7 compare_convert_fusion
  10.7 0.1 copy.17
  10.8 4.9 %copy.24 = f32[1,79,2,4096]{3,1,2,0:T(8,128)} copy(f32[1,79,2,4096]{3,2,1,0:T(2,128)} %param.12) | data formatting | bytes 5177344 | tf_op args[3]
  15.7 2.4 fusion.13
  18.1 0.1 bitcast_divide_fusion
  18.2 0.1 multiply_reduce_fusion.2
  18.3 0.9 fusion.11
  19.1 39.2 %all-reduce.1 = (f32[2]{0:T(128)S(1)}, f32[2,4096]{1,0:T(2,128)S(1)}) all-reduce(f32[2]{0:T(128)S(1)} %fusion.17, f32[2,4096]{1,0:T(2,128)S(1)} %get-tuple-element.10), channel_id=1, replica_groups=mesh['groups'=2,'dp'=8,'mp'=2] {'dp'}, use_global_device_ids=true, to_apply=%region_1.0 | all-reduce | flops 8194 | bytes 65552 | tf_op jit(solution)/shard_map/psum | solution.py:45
  58.3 0.6 fusion.18
  58.9 1.3 fusion.12
  60.2 3.1 fusion.10
  63.4 1.2 pad_maximum_fusion
  64.6 0.7 all-gather.3.cloned.1.call-update
  65.4 4.7 %collective-permute-start.4 = (bf16[1,512,1024]{2,1,0:T(8,128)(2,1)}, bf16[1,512,1024]{2,1,0:T(8,128)(2,1)}, u32[]{:S(2)}, u32[]{:S(2)}) collective-permute-start(bf16[1,512,1024]{2,1,0:T(8,128)(2,1)} %param.15), channel_id=1, source_target_pairs={{0,14},{2,0},{4,2},{6,4},{8,6},{10,8},{12,10},{14,12},{1,15},{3,1}... | collective-permute-start | bytes 3145736 | tf_op jit(solution)/shard_map/ppermute | solution.py:18
  70.1 0.1 broadcast_divide_fusion
  70.2 0.6 multiply_reduce_fusion.3
  71.6 0.6 dynamic-slice.1
  72.8 0.7 fusion.8
  73.6 5.1 %fusion.1 = f32[1024]{0:T(1024)S(1)} fusion(bf16[1,4096,1024]{2,1,0:T(8,128)(2,1)} %param.17, f32[4096]{0:T(1024)S(1)} %bitcast.54), kind=kLoop, calls=%fused_computation.3 | loop fusion | flops 12581888 | bytes 8409088 | tf_op jit(solution)/shard_map/reduce_sum | solution.py:78
  78.7 0.8 maximum_dynamic-update-slice_fusion
  79.4 3.3 all-reduce
  82.7 0.1 reshape.183
  82.8 25.6 %collective-permute-done = bf16[1,512,1024]{2,1,0:T(8,128)(2,1)} collective-permute-done((bf16[1,512,1024]{2,1,0:T(8,128)(2,1)}, bf16[1,512,1024]{2,1,0:T(8,128)(2,1)}, u32[]{:S(2)}, u32[]{:S(2)}) %collective-permute-start) | collective-permute-done | bytes 1048608 | tf_op jit(solution)/shard_map/ppermute | solution.py:15
  108.4 2.5 collective-permute-start.1
  110.8 0.6 slice_reduce_fusion
  112.1 0.1 multiply_reduce_fusion.5
  112.3 23.7 %collective-permute-start.5 = (bf16[1,512,1024]{2,1,0:T(8,128)(2,1)}, bf16[1,512,1024]{2,1,0:T(8,128)(2,1)}, u32[]{:S(2)}, u32[]{:S(2)}) collective-permute-start(bf16[1,512,1024]{2,1,0:T(8,128)(2,1)} %collective-permute-done.4), channel_id=1, source_target_pairs={{0,14},{2,0},{4,2},{6,4},{8,6},{10,8},{12,10},{14,12},{1,15},{3,1}... | collective-permute-start | bytes 3145736 | tf_op jit(solution)/shard_map/ppermute | solution.py:18
  136.0 21.9 %collective-permute-done.1 = bf16[1,512,1024]{2,1,0:T(8,128)(2,1)} collective-permute-done((bf16[1,512,1024]{2,1,0:T(8,128)(2,1)}, bf16[1,512,1024]{2,1,0:T(8,128)(2,1)}, u32[]{:S(2)}, u32[]{:S(2)}) %collective-permute-start.1) | collective-permute-done | bytes 1048608 | tf_op jit(solution)/shard_map/ppermute | solution.py:15
  157.9 2.5 collective-permute-start.2
  160.4 0.1 multiply_reduce_fusion.4
  160.5 1.2 multiply_reduce_fusion
  161.6 49.5 %all-reduce.5.cloned.1.call-done = f32[80,4096]{1,0:T(8,128)} async-done(((f32[80,4096]{1,0:T(8,128)}), f32[80,4096]{1,0:T(8,128)}) %all-reduce.5.cloned.1.call-update) | async-done | bytes 1310736 | tf_op jit(solution)/shard_map/psum | solution.py:68
  211.1 1.5 multiply_reduce_fusion.1
  212.7 2.5 all-reduce.2
  215.1 2.5 collective-permute-start.6
  217.6 1.7 multiply_convert_fusion
  219.3 55.0 %collective-permute-done.3 = bf16[1,512,1024]{2,1,0:T(8,128)(2,1)S(1)} collective-permute-done((bf16[1,512,1024]{2,1,0:T(8,128)(2,1)}, bf16[1,512,1024]{2,1,0:T(8,128)(2,1)S(1)}, u32[]{:S(2)}, u32[]{:S(2)}) %collective-permute-start.3) | collective-permute-done | bytes 1048608 | tf_op jit(solution)/shard_map/ppermute | solution.py:15
  274.3 0.1 constant_dynamic-update-slice_fusion.15
  274.4 1.3 constant_dynamic-update-slice_fusion.14
  275.7 1.3 constant_dynamic-update-slice_fusion.13
  277.0 1.3 constant_dynamic-update-slice_fusion.12
  278.3 0.1 constant_dynamic-update-slice_fusion.11
  278.4 1.3 constant_dynamic-update-slice_fusion.10
  279.7 1.3 constant_dynamic-update-slice_fusion.9
  281.0 0.1 constant_dynamic-update-slice_fusion.8
  281.1 0.1 constant_dynamic-update-slice_fusion.7
  281.1 1.3 constant_dynamic-update-slice_fusion.6
  282.4 1.3 constant_dynamic-update-slice_fusion.5
  283.7 1.3 constant_dynamic-update-slice_fusion.4
  285.0 0.1 constant_dynamic-update-slice_fusion.3
  285.1 1.3 constant_dynamic-update-slice_fusion.2
  286.4 1.3 constant_dynamic-update-slice_fusion.1
  287.7 0.1 constant_dynamic-update-slice_fusion
  287.8 4.7 %fusion.5 = f32[384,1024]{1,0:T(8,128)} fusion(bf16[384,4096]{1,0:T(8,128)(2,1)S(1)} %bitcast.46, bf16[1,8192,1024]{2,1,0:T(8,128)(2,1)S(1)} %constant_dynamic-update-slice_fusion, s32[]{:T(128)S(6)} %select_n.29), kind=kOutput, calls=%fused_computation.7 | convolution fusion | flops 3221225472 | bytes 13107204 | tf_op jit(solution)/shard_map/dot_general | solution.py:96
  292.6 69.2 %all-gather.3.cloned.1.call-done = bf16[1,4096,1024]{2,1,0:T(8,128)(2,1)} async-done(((bf16[1,512,1024]{2,1,0:T(8,128)(2,1)}), bf16[1,4096,1024]{2,1,0:T(8,128)(2,1)}) %all-gather.3.cloned.1.call-update) | async-done | bytes 8388624 | tf_op jit(solution)/shard_map/all_gather | solution.py:67
  361.8 8.9 %fusion.3 = f32[384,1024]{1,0:T(8,128)} fusion(bf16[384,4096]{1,0:T(8,128)(2,1)} %bitcast.47, bf16[1,4096,1024]{2,1,0:T(8,128)(2,1)} %all-gather.3.cloned.1.call-done), kind=kOutput, calls=%fused_computation.5 | convolution fusion | flops 3221225472 | bytes 13107200 | tf_op jit(solution)/shard_map/dot_general | solution.py:97
  370.7 8.0 %fusion.2 = bf16[1,4096,1024]{2,1,0:T(8,128)(2,1)} fusion(bf16[1,4096,1024]{2,1,0:T(8,128)(2,1)} %param.17, f32[1024]{0:T(1024)S(1)} %slice.54, f32[4096]{0:T(1024)S(1)} %bitcast.52), kind=kLoop, calls=%fused_computation.4 | loop fusion | flops 16777216 | bytes 16797696 | tf_op jit(solution)/shard_map/convert_element_type | solution.py:93
  378.7 1.2 broadcast_multiply_fusion
  379.9 2.2 convert_element_type.52
  382.1 1.7 reduce-scatter.5.cloned.1.call-done
  383.8 1.9 convert_element_type.53
  (34 shorter events, 0.4 us)
Async XLA Ops:
  7.2 204.0 %all-reduce.5.cloned.1.call-start = ((), (), s32[]{:S(2)}) async-start(), calls=%async_computation.2 | async-start | bytes 2621440 | tf_op jit(solution)/shard_map/psum | solution.py:68
  10.8 60.8 %copy-start.5 = (u32[32]{0:T(128)S(1)}, u32[32]{0:T(128)}, u32[]{:S(2)}) copy-start(u32[32]{0:T(128)} %constant.80) | copy-start | bytes 388
  10.8 62.1 %copy-start = (bf16[3,128,4096]{2,1,0:T(8,128)(2,1)S(1)}, bf16[3,128,4096]{2,1,0:T(8,128)(2,1)}, u32[]{:S(2)}) copy-start(bf16[3,128,4096]{2,1,0:T(8,128)(2,1)} %param.9) | copy-start | bytes 9437188
  64.6 297.2 %all-gather.3.cloned.1.call-start = ((), (), s32[]{:S(2)}) async-start(), calls=%async_computation.4 | async-start | bytes 9437184 | tf_op jit(solution)/shard_map/all_gather | solution.py:67
  65.3 152.3 %copy-start.4 = (f32[4096]{0:T(1024)S(1)}, f32[4096]{0:T(1024)}, u32[]{:S(2)}) copy-start(f32[4096]{0:T(1024)} %param.14) | copy-start | bytes 49156
  65.3 314.6 %reduce-scatter.3.cloned.1.call-start = ((), (), s32[]{:S(2)}) async-start(), calls=%async_computation.3 | async-start | bytes 2359296 | tf_op jit(solution)/shard_map/reduce_scatter | solution.py:99
  65.4 43.0 %collective-permute-start = (bf16[1,512,1024]{2,1,0:T(8,128)(2,1)}, bf16[1,512,1024]{2,1,0:T(8,128)(2,1)}, u32[]{:S(2)}, u32[]{:S(2)}) collective-permute-start(bf16[1,512,1024]{2,1,0:T(8,128)(2,1)} %param.15), channel_id=1, source_target_pairs={{0,2},{2,4},{4,6},{6,8},{8,10},{10,12},{12,14},{14,0},{1,3},{3,5},... | collective-permute-start | bytes 3145736 | tf_op jit(solution)/shard_map/ppermute | solution.py:15
  65.4 46.9 %collective-permute-start.4 = (bf16[1,512,1024]{2,1,0:T(8,128)(2,1)}, bf16[1,512,1024]{2,1,0:T(8,128)(2,1)}, u32[]{:S(2)}, u32[]{:S(2)}) collective-permute-start(bf16[1,512,1024]{2,1,0:T(8,128)(2,1)} %param.15), channel_id=1, source_target_pairs={{0,14},{2,0},{4,2},{6,4},{8,6},{10,8},{12,10},{14,12},{1,15},{3,1}... | collective-permute-start | bytes 3145736 | tf_op jit(solution)/shard_map/ppermute | solution.py:18
  108.4 49.5 %collective-permute-start.1 = (bf16[1,512,1024]{2,1,0:T(8,128)(2,1)}, bf16[1,512,1024]{2,1,0:T(8,128)(2,1)}, u32[]{:S(2)}, u32[]{:S(2)}) collective-permute-start(bf16[1,512,1024]{2,1,0:T(8,128)(2,1)} %collective-permute-done), channel_id=1, source_target_pairs={{0,2},{2,4},{4,6},{6,8},{8,10},{10,12},{12,14},{14,0},{1,3},{3,5},... | collective-permute-start | bytes 3145736 | tf_op jit(solution)/shard_map/ppermute | solution.py:15
  112.3 102.8 %collective-permute-start.5 = (bf16[1,512,1024]{2,1,0:T(8,128)(2,1)}, bf16[1,512,1024]{2,1,0:T(8,128)(2,1)}, u32[]{:S(2)}, u32[]{:S(2)}) collective-permute-start(bf16[1,512,1024]{2,1,0:T(8,128)(2,1)} %collective-permute-done.4), channel_id=1, source_target_pairs={{0,14},{2,0},{4,2},{6,4},{8,6},{10,8},{12,10},{14,12},{1,15},{3,1}... | collective-permute-start | bytes 3145736 | tf_op jit(solution)/shard_map/ppermute | solution.py:18
  157.9 59.7 %collective-permute-start.2 = (bf16[1,512,1024]{2,1,0:T(8,128)(2,1)}, bf16[1,512,1024]{2,1,0:T(8,128)(2,1)}, u32[]{:S(2)}, u32[]{:S(2)}) collective-permute-start(bf16[1,512,1024]{2,1,0:T(8,128)(2,1)} %collective-permute-done.1), channel_id=1, source_target_pairs={{0,2},{2,4},{4,6},{6,8},{8,10},{10,12},{12,14},{14,0},{1,3},{3,5},... | collective-permute-start | bytes 3145736 | tf_op jit(solution)/shard_map/ppermute | solution.py:15
  215.1 63.2 %copy-start.2 = (bf16[1,512,1024]{2,1,0:T(8,128)(2,1)S(1)}, bf16[1,512,1024]{2,1,0:T(8,128)(2,1)}, u32[]{:S(2)}) copy-start(bf16[1,512,1024]{2,1,0:T(8,128)(2,1)} %param.15) | copy-start | bytes 3145732
  215.1 65.8 %collective-permute-start.6 = (bf16[1,512,1024]{2,1,0:T(8,128)(2,1)}, bf16[1,512,1024]{2,1,0:T(8,128)(2,1)S(1)}, u32[]{:S(2)}, u32[]{:S(2)}) collective-permute-start(bf16[1,512,1024]{2,1,0:T(8,128)(2,1)} %collective-permute-done.5), channel_id=1, source_target_pairs={{0,14},{2,0},{4,2},{6,4},{8,6},{10,8},{12,10},{14,12},{1,15},{3,1}... | collective-permute-start | bytes 3145736 | tf_op jit(solution)/shard_map/ppermute | solution.py:18
  217.6 56.7 %collective-permute-start.3 = (bf16[1,512,1024]{2,1,0:T(8,128)(2,1)}, bf16[1,512,1024]{2,1,0:T(8,128)(2,1)S(1)}, u32[]{:S(2)}, u32[]{:S(2)}) collective-permute-start(bf16[1,512,1024]{2,1,0:T(8,128)(2,1)} %collective-permute-done.2), channel_id=1, source_target_pairs={{0,2},{2,4},{4,6},{6,8},{8,10},{10,12},{12,14},{14,0},{1,3},{3,5},... | collective-permute-start | bytes 3145736 | tf_op jit(solution)/shard_map/ppermute | solution.py:15
  219.3 68.5 %copy-start.3 = (bf16[3,128,4096]{2,1,0:T(8,128)(2,1)}, bf16[3,128,4096]{2,1,0:T(8,128)(2,1)S(1)}, u32[]{:S(2)}) copy-start(bf16[3,128,4096]{2,1,0:T(8,128)(2,1)S(1)} %multiply_convert_fusion) | copy-start | bytes 9437188
  292.5 91.2 %reduce-scatter.5.cloned.1.call-start = ((), (), s32[]{:S(2)}) async-start(), calls=%async_computation.5 | async-start | bytes 2359296 | tf_op jit(solution)/shard_map/reduce_scatter | solution.py:100
  370.7 8.0 %copy-start.1 = (f32[80,4096]{1,0:T(8,128)S(1)}, f32[80,4096]{1,0:T(8,128)}, u32[]{:S(2)}) copy-start(f32[80,4096]{1,0:T(8,128)} %all-reduce.5.cloned.1.call-done) | copy-start | bytes 3932164
Sparse Core Ops, SparseCore 0:
  64.7 146.4 all-reduce.4
  213.5 148.2 all-gather.2
  364.1 7.2 reduce-scatter.2
  373.5 10.2 reduce-scatter.4
